TPU v7x, 32 devices: a whole 2x2x4 slice. The times are simulated.
32 devices in a mesh: lat: 4 (over z), fld: 4 (over y, x), rep: 2 (over core).
Axes of the slice: x: 2, y: 2, z: 4, core: 2. Of those that a mesh axis runs over, the one named last changes fastest.
Arguments:
- field: float32 [12, 1280, 2560], P('fld', ('lat', 'rep')), may hold values from -6 to 6
- wind_zonal: float32 [12, 1280, 2560], P('fld', ('lat', 'rep')), may hold values from -4 to 4
- wind_merid: float32 [12, 1280, 2560], P('fld', ('lat', 'rep')), may hold values from -4 to 4
- band: int32 [12, 2], replicated, may hold values from 0 to 1280, as said below
- waves: int32 [16, 80], replicated, may hold values from -1 to 1279, as said below
- legendre: bfloat16 [16, 1280, 51328], P(('lat', 'fld')), may hold values from -0.15625 to 0.15625
Outputs:
- spectrum: float32 [16, 12, 2, 51328], P(('lat', 'fld'), 'rep')
Inputs may be any that keep to these rules, and one draw needn't show every extreme that they name: band[f, 0] is below 320 and band[f, 1] is above 960, for every field-level. `waves`: every wavenumber 0 to 1279 stands in exactly one slot of one group; -1 marks an empty slot. Wavenumber m takes 1280 - m columns, and the wavenumbers of one group take at most 51240 columns together; some group takes exactly 51240.
All inputs are finite; a program needn't handle non-finite values.
Results may differ from a plain program's by a relative error of at most 0.0056.
Values may be sent and summed in bfloat16 or wider, within the bound.
A program may use at most 256 MiB of HBM per device.

v0:
```python
import functools
import math

import jax
import jax.numpy as jnp
from jax import lax
from jax.experimental import pallas as pl
from jax.experimental.pallas import tpu as pltpu
from jax.sharding import PartitionSpec as P

M = 1280
LANES = 128
WINDOW = 16
TILE = 4096
PAD = 8
CHUNK = 16


def with_halo(value, sides, width):
    for axis, dim in sides:
        peers, length = (lax.axis_size(axis), value.shape[dim])
        up = [(i, (i + 1) % peers) for i in range(peers - 1)]
        down = [(j, i) for i, j in up]
        last = lax.slice_in_dim(value, length - width, length, axis=dim)
        first = lax.slice_in_dim(value, 0, width, axis=dim)
        before = lax.ppermute(last, axis, up)
        after = lax.ppermute(first, axis, down)
        value = jnp.concatenate([before, value, after], axis=dim)
    return value


def dft_matrix(lon_count, wave_count):
    lon_ids = lax.broadcasted_iota(jnp.int32, (lon_count, wave_count), 0)
    wave_ids = lax.broadcasted_iota(jnp.int32, (lon_count, wave_count), 1)
    angles = (lon_ids * wave_ids % lon_count).astype(jnp.float32) * (2.0 * math.pi / lon_count)
    scaling = 1.0 / math.sqrt(lon_count)
    return jnp.concatenate([jnp.cos(angles) * scaling, -jnp.sin(angles) * scaling], axis=1).astype(
        jnp.bfloat16
    )


def tendency(centre, above_row, below_row, zonal_wind, merid_wind):
    eastward = jnp.roll(centre, -1, axis=-1)
    westward = jnp.roll(centre, 1, axis=-1)
    return (
        -(zonal_wind + centre) * (eastward - westward) * 0.5
        - merid_wind * (above_row - below_row) * 0.5
    )


def band_mask(bounds, first_row, row_total):
    row_ids = first_row + lax.broadcasted_iota(jnp.int32, (1, row_total, 1), 1)
    lower_edge = bounds[:, 0][:, None, None]
    upper_edge = bounds[:, 1][:, None, None]
    return ((row_ids >= lower_edge) & (row_ids < upper_edge)).astype(jnp.float32)


def transform_kernel(lon_count, table_ref, grid_ref, out_ref, matrix):
    slots = table_ref.shape[1]
    low_cos, low_sin = table_ref[0], table_ref[1]
    high_cos, high_sin = table_ref[2], table_ref[3]
    for part in range(lon_count // LANES):
        columns = slice(part * LANES, (part + 1) * LANES)
        scaled_cos = high_cos[:, part : part + 1]
        scaled_sin = high_sin[:, part : part + 1]
        matrix[0:slots, columns] = (scaled_cos * low_cos - scaled_sin * low_sin).astype(jnp.bfloat16)
        matrix[slots : 2 * slots, columns] = (-(scaled_sin * low_cos + scaled_cos * low_sin)).astype(
            jnp.bfloat16
        )
    out_ref[...] = lax.dot_general(
        matrix[...], grid_ref[...], (((1,), (1,)), ((), ())), preferred_element_type=jnp.float32
    ).astype(jnp.bfloat16)


def transform(grid_low, waves, lon_count):
    groups, slots = waves.shape
    wave_column = jnp.where(waves >= 0, waves, 0).reshape(1, groups * slots, 1)
    step = jnp.arange(2, dtype=jnp.int32).reshape(2, 1, 1) * (LANES - 1) + 1
    lane = lax.broadcasted_iota(jnp.int32, (1, 1, LANES), 2)
    turns = (wave_column * ((step * lane) % lon_count)) % lon_count
    angles = turns.astype(jnp.float32) * (2.0 * math.pi / lon_count)
    scale = jnp.array([1.0, 1.0 / math.sqrt(lon_count)], jnp.float32).reshape(2, 1, 1)
    tables = jnp.stack([jnp.cos(angles) * scale, jnp.sin(angles) * scale], axis=1)
    tables = tables.reshape(4, groups * slots, LANES)
    rows = grid_low.shape[0]
    return pl.pallas_call(
        functools.partial(transform_kernel, lon_count),
        out_shape=jax.ShapeDtypeStruct((groups * 2 * slots, rows), jnp.bfloat16),
        grid=(groups,),
        in_specs=[
            pl.BlockSpec((4, slots, LANES), lambda g: (0, g, 0)),
            pl.BlockSpec((rows, lon_count), lambda g: (0, 0)),
        ],
        out_specs=pl.BlockSpec((2 * slots, rows), lambda g: (g, 0)),
        scratch_shapes=[pltpu.VMEM((2 * slots, lon_count), jnp.bfloat16)],
        compiler_params=pltpu.CompilerParams(vmem_limit_bytes=32 << 20),
    )(tables, grid_low)


def exchange_kernel(lat_size, fld_size, rep_size, source, target, send_sem, recv_sem, own_sem):
    lat, fld, rep = lax.axis_index("lat"), lax.axis_index("fld"), lax.axis_index("rep")
    groups = lat_size * fld_size
    rows = target.shape[1]
    half = fld_size // rep_size
    to_rep = fld // half
    place = ((fld % half) * lat_size + lat) * rep_size + rep
    own = lat * fld_size + fld
    stays = to_rep == rep

    def sending(hop):
        group = (own + hop) % groups
        return pltpu.make_async_remote_copy(
            src_ref=source.at[pl.ds(pl.multiple_of(group * rows, 16), rows)],
            dst_ref=target.at[place],
            send_sem=send_sem.at[hop],
            recv_sem=recv_sem.at[place],
            device_id=(group // fld_size, group % fld_size, to_rep),
            device_id_type=pl.DeviceIdType.MESH,
        )

    kept = pltpu.make_async_copy(
        source.at[pl.ds(pl.multiple_of(own * rows, 16), rows)], target.at[place], own_sem
    )
    for hop in range(1, groups):
        sending(hop).start()

    @pl.when(stays)
    def _():
        kept.start()

    @pl.when(jnp.logical_not(stays))
    def _():
        sending(0).start()

    @pl.when(stays)
    def _():
        kept.wait()

    @pl.when(jnp.logical_not(stays))
    def _():
        sending(0).wait_send()

    for hop in range(1, groups):
        sending(hop).wait_send()
    for origin in range(target.shape[0]):

        @pl.when(jnp.logical_not(stays & (place == origin)))
        def _():
            pltpu.make_async_remote_copy(
                src_ref=target.at[origin],
                dst_ref=target.at[origin],
                send_sem=send_sem.at[0],
                recv_sem=recv_sem.at[origin],
                device_id=(lat, fld, 1 - rep),
                device_id_type=pl.DeviceIdType.MESH,
            ).wait_recv()


def exchange(spectra, lat_size, fld_size, rep_size):
    rows = spectra.shape[0] // (lat_size * fld_size)
    origins = fld_size // rep_size * lat_size * rep_size
    return pl.pallas_call(
        functools.partial(exchange_kernel, lat_size, fld_size, rep_size),
        out_shape=jax.ShapeDtypeStruct((origins, rows, spectra.shape[1]), spectra.dtype),
        in_specs=[pl.BlockSpec(memory_space=pltpu.VMEM)],
        out_specs=pl.BlockSpec(memory_space=pltpu.VMEM),
        scratch_shapes=[
            pltpu.SemaphoreType.DMA((lat_size * fld_size,)),
            pltpu.SemaphoreType.DMA((origins,)),
            pltpu.SemaphoreType.DMA,
        ],
        compiler_params=pltpu.CompilerParams(has_side_effects=True, vmem_limit_bytes=16 << 20),
    )(spectra)


def legendre_kernel(
    bands, field_count, first, last, received, starts, stops, legendre, out, ordered, total
):
    slots = starts.shape[0]
    row_count = received.shape[2] // field_count
    tile = pl.program_id(0)
    width = out.shape[3]

    @pl.when(tile == 0)
    def _():
        for origin in range(received.shape[0]):
            part, band = divmod(origin, bands)
            for level in range(field_count):
                for side in range(2):
                    row = (part * field_count + level) * 2 + side
                    ordered[row, :, band * row_count : (band + 1) * row_count] = received[
                        origin,
                        side * slots : (side + 1) * slots,
                        level * row_count : (level + 1) * row_count,
                    ]

    total[...] = jnp.zeros_like(total)
    rows = ordered.shape[0]

    @pl.loop(first[tile], last[tile])
    def _(window):
        here = pl.ds(pl.multiple_of(window * WINDOW, WINDOW), WINDOW)
        products = jnp.dot(
            ordered[:, here, :].reshape(rows * WINDOW, ordered.shape[2]),
            legendre[0],
            preferred_element_type=jnp.float32,
        ).reshape(rows, WINDOW, width)
        columns = tile * width + lax.broadcasted_iota(jnp.int32, (WINDOW, width), 1)
        held = (columns >= starts[here, :]) & (columns < stops[here, :])
        total[...] += jnp.sum(jnp.where(held[None], products, 0.0), axis=1)

    for level in range(rows // 2):
        out[0, level] = total[2 * level : 2 * level + 2, :]


def legendre_sums(received, own_waves, legendre, field_count, bands, wave_total):
    slots = own_waves.shape[0]
    counts = jnp.where(own_waves >= 0, wave_total - own_waves, 0)
    lower = lax.broadcasted_iota(jnp.int32, (slots, slots), 1) <= lax.broadcasted_iota(
        jnp.int32, (slots, slots), 0
    )
    stops = jnp.sum(jnp.where(lower, counts[None, :], 0), axis=1)
    starts = stops - counts
    depth, col_count = legendre.shape[1:]
    width = min(TILE, col_count)
    tiles = pl.cdiv(col_count, width)
    edges = jnp.arange(tiles, dtype=jnp.int32)[:, None] * width
    first = jnp.sum((stops[None, :] <= edges).astype(jnp.int32), axis=1) // WINDOW
    begun = jnp.sum((starts[None, :] < edges + width).astype(jnp.int32), axis=1)
    last = (begun + WINDOW - 1) // WINDOW
    rows = received.shape[0] // bands * field_count * 2
    return pl.pallas_call(
        functools.partial(legendre_kernel, bands, field_count),
        out_shape=jax.ShapeDtypeStruct((1, rows // 2, 2, col_count), jnp.float32),
        grid_spec=pltpu.PrefetchScalarGridSpec(
            num_scalar_prefetch=2,
            grid=(tiles,),
            in_specs=[
                pl.BlockSpec(
                    received.shape, lambda t, *_: (0, 0, 0), pipeline_mode=pl.Buffered(1)
                ),
                pl.BlockSpec((slots, 1), lambda t, *_: (0, 0)),
                pl.BlockSpec((slots, 1), lambda t, *_: (0, 0)),
                pl.BlockSpec((1, depth, width), lambda t, *_: (0, 0, t)),
            ],
            out_specs=pl.BlockSpec((1, rows // 2, 2, width), lambda t, *_: (0, 0, 0, t)),
            scratch_shapes=[
                pltpu.VMEM((rows, slots, depth), jnp.bfloat16),
                pltpu.VMEM((rows, width), jnp.float32),
            ],
        ),
        compiler_params=pltpu.CompilerParams(vmem_limit_bytes=56 << 20),
    )(first, last, received, starts[:, None], stops[:, None], legendre)


def advection_kernel(bounds, origin, field, zonal, merid, above, below, out, edges, padded, section):
    level = pl.program_id(0)
    rows = field.shape[1]
    length = field.shape[2]
    lower, upper, start = bounds[level, 0], bounds[level, 1], origin[0]

    def masked_slope(first_row, centre, turned_east, turned_west, next_row, previous, zonal_wind, merid_wind):
        row_ids = start + first_row + lax.broadcasted_iota(jnp.int32, centre.shape, 0)
        in_band = ((row_ids >= lower) & (row_ids < upper)).astype(jnp.float32)
        return in_band * (
            -(zonal_wind + centre) * (turned_east - turned_west) * 0.5
            - merid_wind * (next_row - previous) * 0.5
        )

    def turned(value):
        return pltpu.roll(value, length - 1, axis=1), pltpu.roll(value, 1, axis=1)

    padded[PAD : PAD + rows, :] = field[0]
    padded[PAD - 2 : PAD, :] = above[0, 0:2, :]
    padded[PAD + rows : PAD + rows + 2, :] = below[0, 0:2, :]
    edges[0:4, :] = above[0]
    edges[4:8, :] = below[0]
    halo = edges[...]
    east, west = turned(halo)
    section[PAD - 1 : PAD, :] = halo[1:2] + masked_slope(
        -1, halo[1:2], east[1:2], west[1:2], field[0, 0:1, :], halo[0:1], halo[2:3], halo[3:4]
    )
    section[PAD + rows : PAD + rows + 1, :] = halo[4:5] + masked_slope(
        rows, halo[4:5], east[4:5], west[4:5], halo[5:6], field[0, rows - 1 : rows, :], halo[6:7], halo[7:8]
    )

    def neighbours(ref, first_row):
        value = ref[pl.ds(first_row, 2 * PAD + CHUNK), :]
        return tuple(value[PAD + shift : PAD + shift + CHUNK] for shift in (-1, 0, 1))

    @pl.loop(0, rows // CHUNK)
    def _(chunk):
        first_row = pl.multiple_of(chunk * CHUNK, CHUNK)
        here = pl.ds(first_row, CHUNK)
        previous, centre, next_row = neighbours(padded, first_row)
        section[pl.ds(pl.multiple_of(first_row + PAD, PAD), CHUNK), :] = centre + masked_slope(
            first_row, centre, *turned(centre), next_row, previous, zonal[0, here, :], merid[0, here, :]
        )

    @pl.loop(0, rows // CHUNK)
    def _(chunk):
        first_row = pl.multiple_of(chunk * CHUNK, CHUNK)
        here = pl.ds(first_row, CHUNK)
        previous, centre, next_row = neighbours(section, first_row)
        out[0, here, :] = (
            0.5
            * (
                field[0, here, :]
                + centre
                + masked_slope(
                    first_row, centre, *turned(centre), next_row, previous, zonal[0, here, :], merid[0, here, :]
                )
            )
        ).astype(jnp.bfloat16)


def advection(field, wind_zonal, wind_merid, bounds, first_row):
    levels, rows, length = field.shape
    peers = lax.axis_size(("lat", "rep"))
    up = [(i, i + 1) for i in range(peers - 1)]
    down = [(i + 1, i) for i in range(peers - 1)]
    winds = (wind_zonal, wind_merid)
    above = lax.ppermute(
        jnp.concatenate([field[:, -2:]] + [w[:, -1:] for w in winds], axis=1), ("lat", "rep"), up
    )
    below = lax.ppermute(
        jnp.concatenate([field[:, :2]] + [w[:, :1] for w in winds], axis=1), ("lat", "rep"), down
    )
    whole = pl.BlockSpec((1, rows, length), lambda f, *_: (f, 0, 0))
    edge = pl.BlockSpec((1, 4, length), lambda f, *_: (f, 0, 0))
    return pl.pallas_call(
        advection_kernel,
        out_shape=jax.ShapeDtypeStruct(field.shape, jnp.bfloat16),
        grid_spec=pltpu.PrefetchScalarGridSpec(
            num_scalar_prefetch=2,
            grid=(levels,),
            in_specs=[whole, whole, whole, edge, edge],
            out_specs=whole,
            scratch_shapes=[
                pltpu.VMEM((8, length), jnp.float32),
                pltpu.VMEM((rows + 2 * PAD, length), jnp.float32),
                pltpu.VMEM((rows + 2 * PAD, length), jnp.float32),
            ],
        ),
        compiler_params=pltpu.CompilerParams(vmem_limit_bytes=60 << 20),
    )(bounds, first_row.reshape(1), field, wind_zonal, wind_merid, above, below)


def body(field, wind_zonal, wind_merid, band, waves, legendre):
    field_count, row_count, lon_count = field.shape
    lat_size = lax.axis_size("lat")
    fld_size = lax.axis_size("fld")
    rep_size = lax.axis_size("rep")
    first_row = (lax.axis_index("lat") * rep_size + lax.axis_index("rep")) * row_count
    bounds = lax.dynamic_slice_in_dim(band, lax.axis_index("fld") * field_count, field_count, 0)
    slot_count = waves.shape[1]
    direct = (
        row_count % 16 == 0
        and slot_count % WINDOW == 0
        and lon_count % LANES == 0
        and lon_count // LANES <= LANES
        and fld_size % rep_size == 0
        and lat_size * fld_size <= 64
    )
    if direct:
        grid_low = advection(field, wind_zonal, wind_merid, bounds, first_row)
        spectra = transform(
            grid_low.reshape(field_count * row_count, lon_count), waves, lon_count
        )
        received = exchange(spectra, lat_size, fld_size, rep_size)
        group = lax.axis_index("lat") * fld_size + lax.axis_index("fld")
        own_waves = lax.dynamic_index_in_dim(waves, group, 0, keepdims=False)
        return legendre_sums(
            received, own_waves, legendre, field_count, lat_size * rep_size, M
        )
    in_band = band_mask(bounds, first_row, row_count)
    padded = with_halo(field, ((("lat", "rep"), 1),), 1)
    first_section = field + in_band * tendency(
        field, padded[:, 2:], padded[:, :-2], wind_zonal, wind_merid
    )
    padded_section = with_halo(first_section, ((("lat", "rep"), 1),), 1)
    advected = 0.5 * (
        field
        + first_section
        + in_band
        * tendency(
            first_section, padded_section[:, 2:], padded_section[:, :-2], wind_zonal, wind_merid
        )
    )
    grid_low = advected.astype(jnp.bfloat16)
    spectra = jnp.dot(
        grid_low.reshape(field_count * row_count, lon_count),
        dft_matrix(lon_count, M),
        preferred_element_type=jnp.float32,
    ).astype(jnp.bfloat16)
    spectra = spectra.reshape(field_count, row_count, 2, M)
    wave_index = jnp.where(waves >= 0, waves, 0)
    picked = jnp.take(spectra, wave_index.reshape(-1), axis=3)
    picked = picked.reshape(field_count, row_count, 2, lat_size, fld_size, slot_count)
    outgoing = jnp.transpose(picked, (5, 2, 4, 0, 3, 1)).reshape(
        slot_count, 2, fld_size * field_count, lat_size * row_count
    )
    received = lax.all_to_all(
        lax.all_to_all(outgoing, "lat", split_axis=3, concat_axis=3, tiled=True),
        "fld",
        split_axis=2,
        concat_axis=2,
        tiled=True,
    )
    group = lax.axis_index("lat") * fld_size + lax.axis_index("fld")
    own_waves = lax.dynamic_index_in_dim(waves, group, 0, keepdims=False)
    counts = jnp.where(own_waves >= 0, M - own_waves, 0)
    offsets = jnp.cumsum(counts) - counts
    col_count = legendre.shape[2]
    col_ids = lax.broadcasted_iota(jnp.int32, (slot_count, col_count), 1)
    segments = ((col_ids >= offsets[:, None]) & (col_ids < (offsets + counts)[:, None])).astype(
        jnp.float32
    )
    total_fields = fld_size * field_count
    regrouped = lax.all_to_all(received, "rep", split_axis=2, concat_axis=3, tiled=True)
    half_fields = total_fields // rep_size
    ordered = regrouped.reshape(slot_count, 2, half_fields, rep_size, lat_size, row_count)
    ordered = jnp.transpose(ordered, (0, 1, 2, 4, 3, 5)).reshape(
        slot_count * 2 * half_fields, rep_size * lat_size * row_count
    )
    products = jnp.dot(ordered, legendre[0], preferred_element_type=jnp.float32)
    spectrum = jnp.einsum(
        "scfk,sk->fck", products.reshape(slot_count, 2, half_fields, col_count), segments
    )
    return spectrum[None]


def solution(mesh):
    placed = (
        P("fld", ("lat", "rep"), None),
        P("fld", ("lat", "rep"), None),
        P("fld", ("lat", "rep"), None),
        P(),
        P(),
        P(("lat", "fld"), None, None),
    )
    return jax.shard_map(
        body,
        mesh=mesh,
        in_specs=placed,
        out_specs=P(("lat", "fld"), "rep", None, None),
        check_vma=False,
    )
```

profile of v0, /device:TPU:15, one launch (start us, length us, event | category | flops | bytes accessed | tf_op | source)
XLA Modules:
  0.0 186.6 jit_solution(5865267298916720872)
XLA Ops:
  0.0 0.0 copy-start
  0.0 1.1 fusion.6
  1.1 1.4 fusion.7
  2.5 0.1 pad_maximum_fusion.1
  2.6 3.8 %collective-permute-start = (f32[3,4,2560]{2,1,0:T(4,128)S(1)}, f32[3,4,2560]{2,1,0:T(4,128)S(1)}, u32[]{:S(2)}, u32[]{:S(2)}) collective-permute-start(f32[3,4,2560]{2,1,0:T(4,128)S(1)} %pad_maximum_fusion.1), channel_id=1, source_target_pairs={{0,1},{1,8},{8,9},{9,16},{16,17},{17,24},{24,25},{2,3},{3,10},{10,... | collective-permute-start | bytes 368648 | tf_op jit(solution)/shard_map/ppermute | solution.py:323
  6.4 0.1 pad_maximum_fusion.2
  6.5 1.9 %collective-permute-start.1 = (f32[3,4,2560]{2,1,0:T(4,128)S(1)}, f32[3,4,2560]{2,1,0:T(4,128)S(1)}, u32[]{:S(2)}, u32[]{:S(2)}) collective-permute-start(f32[3,4,2560]{2,1,0:T(4,128)S(1)} %pad_maximum_fusion.2), channel_id=1, source_target_pairs={{1,0},{8,1},{9,8},{16,9},{17,16},{24,17},{25,24},{3,2},{10,3},{11,... | collective-permute-start | bytes 368648 | tf_op jit(solution)/shard_map/ppermute | solution.py:326
  8.5 0.7 compare_select_fusion
  9.2 0.7 fusion.9
  9.9 0.1 select_reduce_fusion
  10.0 0.7 fusion.5
  10.7 0.7 bitcast_subtract_fusion
  11.4 0.2 convert_reduce_fusion.1
  11.5 0.1 and_select_fusion
  11.6 0.1 mul.124
  11.7 0.0 copy-done
  11.7 0.1 constant_dynamic-slice_fusion
  11.8 0.7 copy.19.bounds
  12.5 0.7 copy.17.starts
  13.2 0.7 copy.18.stops
  13.9 0.2 convert_reduce_fusion
  14.1 6.1 %cosine_multiply_fusion = (f32[2,1,1280,128]{3,2,1,0:T(8,128)S(1)}, f32[2,1,1280,128]{3,2,1,0:T(8,128)S(1)}) fusion(f32[2]{0:T(128)} %constant.83.clone, s32[2,128]{1,0:T(2,128)S(1)} %and_select_fusion, s32[1280]{0:T(1024)S(1)} %mul.124), kind=kLoop, calls=%fused_computation.5 | loop fusion | flops 3604480 | bytes 2627592 | tf_op jit(solution)/shard_map/mul | solution.py:83
  20.1 0.2 pad_maximum_fusion
  20.3 0.6 and_select_fusion.1
  20.9 0.0 collective-permute-done.above
  20.9 0.0 copy-start.3
  20.9 0.0 collective-permute-done.1.below
  20.9 0.0 copy-start.4
  20.9 0.6 copy-done.3
  21.6 0.0 copy-done.4
  21.6 15.3 %shard_map.73 = bf16[3,160,2560]{2,1,0:T(8,128)(2,1)} custom-call(s32[3,2]{1,0:T(4,128)} %copy.19.bounds, s32[1]{0:T(128)} %bitcast.4.origin, f32[3,160,2560]{2,1,0:T(8,128)} %field.1, f32[3,160,2560]{2,1,0:T(8,128)} %zonal.1, f32[3,160,2560]{2,1,0:T(8,128)} %merid.1, f32[3,4,2560]{2,1,0:T(4,128)} %copy-done.3, f32[3,4,2560]{2,1,0:T(4,128)} %copy-done.4), custom_call_target="tpu_custom_call" | custom-call | tf_op jit(solution)/shard_map/pallas_call | solution.py:331
  36.9 0.0 copy-start.2
  36.9 1.7 copy-done.2
  38.6 16.0 %shard_map.74.source = bf16[2560,480]{1,0:T(8,128)(2,1)S(1)} custom-call(f32[4,1280,128]{2,1,0:T(8,128)S(1)} %bitcast.15, bf16[480,2560]{1,0:T(8,128)(2,1)S(1)} %bitcast.16), custom_call_target="tpu_custom_call" | custom-call | tf_op jit(solution)/shard_map/pallas_call | solution.py:86
  54.6 73.5 %shard_map.75.received = bf16[16,160,480]{2,1,0:T(8,128)(2,1)S(1)} custom-call(bf16[2560,480]{1,0:T(8,128)(2,1)S(1)} %shard_map.74.source), custom_call_target="tpu_custom_call" | custom-call | tf_op jit(solution)/shard_map/pallas_call | solution.py:162
  128.1 0.0 copy-start.1
  128.1 1.5 copy-done.1
  129.6 57.0 %shard_map.76 = f32[1,6,2,51328]{3,2,1,0:T(2,128)} custom-call(s32[13]{0:T(128)} %get-tuple-element.14.first, s32[13]{0:T(128)} %get-tuple-element.13.last, bf16[16,160,480]{2,1,0:T(8,128)(2,1)} %copy-done.1, s32[80,1]{1,0:T(8,128)} %copy.17.starts, s32[80,1]{1,0:T(8,128)} %copy.18.stops, bf16[1,1280,51328]{2,1,0:T(8,128)(2,1)} %legendre.1), custom_call_target="tpu_custom_call" | custom-call | tf_op jit(solution)/shard_map/pallas_call | solution.py:232
  (3 shorter events, 0.0 us)
Async XLA Ops:
  0.0 11.7 %copy-start = (s32[12,2]{0,1:T(2,128)S(1)}, s32[12,2]{0,1:T(2,128)}, u32[]{:S(2)}) copy-start(s32[12,2]{0,1:T(2,128)} %param.10) | copy-start | bytes 292
  2.6 18.3 %collective-permute-start = (f32[3,4,2560]{2,1,0:T(4,128)S(1)}, f32[3,4,2560]{2,1,0:T(4,128)S(1)}, u32[]{:S(2)}, u32[]{:S(2)}) collective-permute-start(f32[3,4,2560]{2,1,0:T(4,128)S(1)} %pad_maximum_fusion.1), channel_id=1, source_target_pairs={{0,1},{1,8},{8,9},{9,16},{16,17},{17,24},{24,25},{2,3},{3,10},{10,... | collective-permute-start | bytes 368648 | tf_op jit(solution)/shard_map/ppermute | solution.py:323
  6.5 14.4 %collective-permute-start.1 = (f32[3,4,2560]{2,1,0:T(4,128)S(1)}, f32[3,4,2560]{2,1,0:T(4,128)S(1)}, u32[]{:S(2)}, u32[]{:S(2)}) collective-permute-start(f32[3,4,2560]{2,1,0:T(4,128)S(1)} %pad_maximum_fusion.2), channel_id=1, source_target_pairs={{1,0},{8,1},{9,8},{16,9},{17,16},{24,17},{25,24},{3,2},{10,3},{11,... | collective-permute-start | bytes 368648 | tf_op jit(solution)/shard_map/ppermute | solution.py:326
  20.9 0.6 copy-start.3
  20.9 0.7 copy-start.4
  36.9 1.7 copy-start.2
  128.1 1.5 copy-start.1
where the time goes:
time: 187 us
  Pallas kernels  162 us (87%)
  other arithmetic  10.4 us (6%)
  local copies, waits for them, and re-layouts  8.64 us (5%)
  starting transfers between devices  5.69 us (3%)
    pallas_call x1, Pallas kernels, exchange(): pl.pallas_call(functools.partial(exchange_kernel, lat_size, fld_size, rep...  73.5 us
    pallas_call x1, Pallas kernels, legendre_sums(): pl.pallas_call(functools.partial(legendre_kernel, bands, field_count), ou...  57 us
    pallas_call x1, Pallas kernels, transform(): pl.pallas_call(functools.partial(transform_kernel, lon_count), out_shape=...  16 us
    pallas_call x1, Pallas kernels, advection(): pl.pallas_call(advection_kernel, out_shape=jax.ShapeDtypeStruct(field.sha...  15.3 us
    mul x1, other arithmetic, transform(): jnp.cos(angles) * scale  6.06 us
    unnamed x11, local copies, waits for them, and re-layouts  4.55 us
    ppermute x1, starting transfers between devices, advection(): lax.ppermute(jnp.concatenate([field[:, -2:]] + [w[:, -1:] for w in winds]...  3.77 us
  transfers between devices with their start and end apart: 2, of which 0 were waited for; matrix products, arithmetic and copies ran while one was open for 7% of the time, Pallas kernels for 0%

commit v1 on v0

v1 whole, which is shorter than its diff:
```python
import functools
import math

import jax
import jax.numpy as jnp
from jax import lax
from jax.experimental import pallas as pl
from jax.experimental.pallas import tpu as pltpu
from jax.sharding import PartitionSpec as P

M = 1280
LANES = 128
PAD = 8
CHUNK = 16


def with_halo(value, sides, width):
    for axis, dim in sides:
        peers, length = (lax.axis_size(axis), value.shape[dim])
        up = [(i, (i + 1) % peers) for i in range(peers - 1)]
        down = [(j, i) for i, j in up]
        last = lax.slice_in_dim(value, length - width, length, axis=dim)
        first = lax.slice_in_dim(value, 0, width, axis=dim)
        before = lax.ppermute(last, axis, up)
        after = lax.ppermute(first, axis, down)
        value = jnp.concatenate([before, value, after], axis=dim)
    return value


def dft_matrix(lon_count, wave_count):
    lon_ids = lax.broadcasted_iota(jnp.int32, (lon_count, wave_count), 0)
    wave_ids = lax.broadcasted_iota(jnp.int32, (lon_count, wave_count), 1)
    angles = (lon_ids * wave_ids % lon_count).astype(jnp.float32) * (2.0 * math.pi / lon_count)
    scaling = 1.0 / math.sqrt(lon_count)
    return jnp.concatenate([jnp.cos(angles) * scaling, -jnp.sin(angles) * scaling], axis=1).astype(
        jnp.bfloat16
    )


def tendency(centre, above_row, below_row, zonal_wind, merid_wind):
    eastward = jnp.roll(centre, -1, axis=-1)
    westward = jnp.roll(centre, 1, axis=-1)
    return (
        -(zonal_wind + centre) * (eastward - westward) * 0.5
        - merid_wind * (above_row - below_row) * 0.5
    )


def band_mask(bounds, first_row, row_total):
    row_ids = first_row + lax.broadcasted_iota(jnp.int32, (1, row_total, 1), 1)
    lower_edge = bounds[:, 0][:, None, None]
    upper_edge = bounds[:, 1][:, None, None]
    return ((row_ids >= lower_edge) & (row_ids < upper_edge)).astype(jnp.float32)


SUB = 256
WIDE = 4096
HELD = 2


def angle_tables(waves, lon_count):
    groups, slots = waves.shape
    wave_column = jnp.where(waves >= 0, waves, 0).reshape(groups * slots, 1)
    lane = lax.broadcasted_iota(jnp.int32, (1, LANES), 1)
    quarter = lon_count // 4

    def cos_sin(step, scale):
        turns = (wave_column * ((step * lane) % lon_count)) % lon_count
        nearest = (2 * turns + quarter) // (2 * quarter)
        angle = (turns - nearest * quarter).astype(jnp.float32) * (2.0 * math.pi / lon_count)
        square = angle * angle
        cosine = 1.0 + square * (
            -0.5 + square * (1.0 / 24 + square * (-1.0 / 720 + square * (1.0 / 40320 - square / 3628800)))
        )
        sine = angle * (
            1.0 + square * (-1.0 / 6 + square * (1.0 / 120 + square * (-1.0 / 5040 + square / 362880)))
        )
        turn = nearest % 4
        odd = turn % 2 == 1
        cos_sign = jnp.where((turn == 1) | (turn == 2), -scale, scale)
        sin_sign = jnp.where(turn >= 2, -scale, scale)
        return jnp.where(odd, sine, cosine) * cos_sign, jnp.where(odd, cosine, sine) * sin_sign

    return cos_sin(1, 1.0) + cos_sin(LANES, 1.0 / math.sqrt(lon_count))


def spread_kernel(
    sizes, cuts, band, edges, low_cos, low_sin, high_cos, high_sin, field, zonal_in, merid_in, received,
    padded, zonal, merid, halo, halo_edges, section, grid_low, matrix, staged,
    load_sem, halo_send, halo_recv, send_sem, recv_sem,
):
    lat_size, fld_size, rep_size = sizes
    lat, fld, rep = lax.axis_index("lat"), lax.axis_index("fld"), lax.axis_index("rep")
    levels, rows, length = zonal.shape
    slots = matrix.shape[1] // 2
    groups = lat_size * fld_size
    half = lat_size // 2
    place = lat * fld_size + fld
    own_band = lat * rep_size + rep
    bands = lat_size * rep_size
    start = own_band * rows

    def load(level, which):
        ref, into = (
            (field, padded.at[level, pl.ds(PAD, rows)]),
            (zonal_in, zonal.at[level]),
            (merid_in, merid.at[level]),
        )[which]
        return pltpu.make_async_copy(ref.at[level], into, load_sem.at[level, which])

    for level in range(levels):
        for which in range(3):
            load(level, which).start()

    def halo_copy(side):
        other = own_band + (1 if side == 0 else -1)
        return pltpu.make_async_remote_copy(
            src_ref=edges.at[side],
            dst_ref=halo.at[side],
            send_sem=halo_send.at[side],
            recv_sem=halo_recv.at[side],
            device_id=(other // rep_size, fld, other % rep_size),
            device_id_type=pl.DeviceIdType.MESH,
        )

    is_first, is_last = own_band == 0, own_band == bands - 1

    @pl.when(jnp.logical_not(is_last))
    def _():
        halo_copy(0).start()

    @pl.when(jnp.logical_not(is_first))
    def _():
        halo_copy(1).start()

    @pl.when(is_first)
    def _():
        halo[0] = jnp.zeros(halo.shape[1:], halo.dtype)

    @pl.when(is_last)
    def _():
        halo[1] = jnp.zeros(halo.shape[1:], halo.dtype)

    @pl.when(jnp.logical_not(is_first))
    def _():
        halo_copy(0).wait_recv()

    @pl.when(jnp.logical_not(is_last))
    def _():
        halo_copy(1).wait_recv()

    def turned(value):
        return pltpu.roll(value, length - 1, axis=1), pltpu.roll(value, 1, axis=1)

    def neighbours(ref, first_row):
        value = ref[pl.ds(first_row, 2 * PAD + CHUNK), :]
        return tuple(value[PAD + shift : PAD + shift + CHUNK] for shift in (-1, 0, 1))

    def advect(level):
        for which in range(3):
            load(level, which).wait()
        lower = band[fld * levels + level, 0]
        upper = band[fld * levels + level, 1]

        def masked_slope(
            first_row, centre, turned_east, turned_west, next_row, previous, zonal_wind, merid_wind
        ):
            row_ids = start + first_row + lax.broadcasted_iota(jnp.int32, centre.shape, 0)
            in_band = ((row_ids >= lower) & (row_ids < upper)).astype(jnp.float32)
            return in_band * (
                -(zonal_wind + centre) * (turned_east - turned_west) * 0.5
                - merid_wind * (next_row - previous) * 0.5
            )

        here_padded = padded.at[level]
        here_padded[PAD - 2 : PAD, :] = halo[0, level, 0:2, :]
        here_padded[PAD + rows : PAD + rows + 2, :] = halo[1, level, 0:2, :]
        halo_edges[0:4, :] = halo[0, level]
        halo_edges[4:8, :] = halo[1, level]
        around = halo_edges[...]
        east, west = turned(around)
        section[PAD - 1 : PAD, :] = around[1:2] + masked_slope(
            -1, around[1:2], east[1:2], west[1:2], here_padded[PAD : PAD + 1, :], around[0:1],
            around[2:3], around[3:4],
        )
        section[PAD + rows : PAD + rows + 1, :] = around[4:5] + masked_slope(
            rows, around[4:5], east[4:5], west[4:5], around[5:6],
            here_padded[PAD + rows - 1 : PAD + rows, :], around[6:7], around[7:8],
        )

        @pl.loop(0, rows // CHUNK)
        def _(chunk):
            first_row = pl.multiple_of(chunk * CHUNK, CHUNK)
            here = pl.ds(first_row, CHUNK)
            previous, centre, next_row = neighbours(here_padded, first_row)
            section[pl.ds(pl.multiple_of(first_row + PAD, PAD), CHUNK), :] = centre + masked_slope(
                first_row, centre, *turned(centre), next_row, previous,
                zonal[level, here, :], merid[level, here, :],
            )

        @pl.loop(0, rows // CHUNK)
        def _(chunk):
            first_row = pl.multiple_of(chunk * CHUNK, CHUNK)
            here = pl.ds(first_row, CHUNK)
            previous, centre, next_row = neighbours(section, first_row)
            grid_low[pl.ds(pl.multiple_of(level * rows + first_row, CHUNK), CHUNK), :] = (
                0.5
                * (
                    here_padded[pl.ds(pl.multiple_of(first_row + PAD, PAD), CHUNK), :]
                    + centre
                    + masked_slope(
                        first_row, centre, *turned(centre), next_row, previous,
                        zonal[level, here, :], merid[level, here, :],
                    )
                )
            ).astype(jnp.bfloat16)

    def target_of(hop):
        turn = hop // fld_size
        crossing = turn < half
        side = jnp.where(crossing, 1 - lat // half, lat // half)
        within = jnp.where(crossing, lat + turn, lat + 1 + turn) % half
        return side * half + within, (fld + 1 + hop % fld_size) % fld_size

    def sending(hop, cut):
        to_lat, to_fld = target_of(hop)
        lanes = pl.ds(cuts[cut], cuts[cut + 1] - cuts[cut])
        return pltpu.make_async_remote_copy(
            src_ref=staged.at[hop, :, lanes],
            dst_ref=received.at[place, :, lanes],
            send_sem=send_sem.at[hop, cut],
            recv_sem=recv_sem.at[place, cut],
            device_id=(to_lat, to_fld, rep),
            device_id_type=pl.DeviceIdType.MESH,
        )

    def build(hop):
        to_lat, to_fld = target_of(hop)
        own_rows = pl.ds(pl.multiple_of((to_lat * fld_size + to_fld) * slots, 8), slots)
        near_cos, near_sin = low_cos[own_rows, :], low_sin[own_rows, :]
        far_cos, far_sin = high_cos[own_rows, :], high_sin[own_rows, :]
        for part in range(length // LANES):
            columns = slice(part * LANES, (part + 1) * LANES)
            scaled_cos = far_cos[:, part : part + 1]
            scaled_sin = far_sin[:, part : part + 1]
            matrix[hop, 0:slots, columns] = (
                scaled_cos * near_cos - scaled_sin * near_sin
            ).astype(jnp.bfloat16)
            matrix[hop, slots : 2 * slots, columns] = (
                -(scaled_sin * near_cos + scaled_cos * near_sin)
            ).astype(jnp.bfloat16)

    done = 0
    for cut in range(len(cuts) - 1):
        lanes = slice(cuts[cut], cuts[cut + 1])
        while done * rows < cuts[cut + 1]:
            advect(done)
            done += 1

        def step(hop, carry, cut=cut, lanes=lanes):
            if cut == 0:
                build(hop)
            staged[hop, :, lanes] = lax.dot_general(
                matrix[hop], grid_low[lanes, :], (((1,), (1,)), ((), ())),
                preferred_element_type=jnp.float32,
            ).astype(jnp.bfloat16)

            @pl.when(hop > 0)
            def _():
                sending(hop - 1, cut).start()

            return carry

        lax.fori_loop(0, groups, step, 0)
        received[place, :, lanes] = staged[groups - 1, :, lanes]

    @pl.when(jnp.logical_not(is_last))
    def _():
        halo_copy(0).wait_send()

    @pl.when(jnp.logical_not(is_first))
    def _():
        halo_copy(1).wait_send()

    for cut in range(len(cuts) - 1):

        def sent(hop, carry, cut=cut):
            sending(hop, cut).wait_send()
            return carry

        lax.fori_loop(0, groups - 1, sent, 0)
    for cut in range(len(cuts) - 1):
        lanes = pl.ds(cuts[cut], cuts[cut + 1] - cuts[cut])

        def arrived(step, carry, cut=cut, lanes=lanes):
            origin = (place + step) % groups
            pltpu.make_async_remote_copy(
                src_ref=staged.at[0, :, lanes],
                dst_ref=received.at[origin, :, lanes],
                send_sem=send_sem.at[0, cut],
                recv_sem=recv_sem.at[origin, cut],
                device_id=(lat, fld, 1 - rep),
                device_id_type=pl.DeviceIdType.MESH,
            ).wait_recv()
            return carry

        lax.fori_loop(1, groups, arrived, 0)


def spread(field, wind_zonal, wind_merid, band, waves, sizes):
    levels, rows, length = field.shape
    groups, slots = waves.shape
    winds = (wind_zonal, wind_merid)
    edges = jnp.stack(
        [
            jnp.concatenate([field[:, -2:]] + [w[:, -1:] for w in winds], axis=1),
            jnp.concatenate([field[:, :2]] + [w[:, :1] for w in winds], axis=1),
        ]
    )
    tables = angle_tables(waves, length)
    width = levels * rows
    full = width // LANES * LANES
    cuts = (0, LANES, 2 * LANES, width) if full >= 3 * LANES else (0, width)
    in_vmem = pl.BlockSpec(memory_space=pltpu.VMEM)
    in_hbm = pl.BlockSpec(memory_space=pl.ANY)
    return pl.pallas_call(
        functools.partial(spread_kernel, sizes, cuts),
        out_shape=jax.ShapeDtypeStruct((groups, 2 * slots, width), jnp.bfloat16),
        in_specs=[pl.BlockSpec(memory_space=pltpu.SMEM)] + [in_vmem] * 5 + [in_hbm] * 3,
        out_specs=in_vmem,
        scratch_shapes=[
            pltpu.VMEM((levels, rows + 2 * PAD, length), jnp.float32),
            pltpu.VMEM((levels, rows, length), jnp.float32),
            pltpu.VMEM((levels, rows, length), jnp.float32),
            pltpu.VMEM((2, levels, 4, length), jnp.float32),
            pltpu.VMEM((8, length), jnp.float32),
            pltpu.VMEM((rows + 2 * PAD, length), jnp.float32),
            pltpu.VMEM((width, length), jnp.bfloat16),
            pltpu.VMEM((groups, 2 * slots, length), jnp.bfloat16),
            pltpu.VMEM((groups, 2 * slots, width), jnp.bfloat16),
            pltpu.SemaphoreType.DMA((levels, 3)),
            pltpu.SemaphoreType.DMA((2,)),
            pltpu.SemaphoreType.DMA((2,)),
            pltpu.SemaphoreType.DMA((groups, len(cuts) - 1)),
            pltpu.SemaphoreType.DMA((groups, len(cuts) - 1)),
        ],
        compiler_params=pltpu.CompilerParams(has_side_effects=True, vmem_limit_bytes=52 << 20),
    )(band, edges, *tables, field, wind_zonal, wind_merid)


def legendre_kernel(
    lat_size, fld_size, field_count, first, last, starts, stops, own_rep, received, legendre,
    mine, theirs, ordered,
):
    tile = pl.program_id(0)
    width = mine.shape[1]
    slots = received.shape[1] // 2
    row_count = received.shape[2] // field_count
    depth = lat_size * row_count
    rows = fld_size * field_count * 2
    kept = rows // 2
    subs = width // SUB

    @pl.when(tile == 0)
    def _():
        for part in range(fld_size):
            fld = (part + own_rep[0] * (fld_size // 2)) % fld_size
            for level in range(field_count):
                for side in range(2):
                    row = (part * field_count + level) * 2 + side
                    piece = jnp.concatenate(
                        [
                            received[
                                lat * fld_size + fld,
                                side * slots : (side + 1) * slots,
                                level * row_count : (level + 1) * row_count,
                            ].astype(jnp.float32)
                            for lat in range(lat_size)
                        ],
                        axis=1,
                    )
                    for lane in range(depth // LANES):
                        ordered[lane, pl.ds(row, slots, stride=rows), :] = piece[
                            :, lane * LANES : (lane + 1) * LANES
                        ]

    def held(slot, columns):
        return (columns >= starts[slot]) & (columns < stops[slot])

    def taken(slot):
        at = jnp.minimum(slot, slots - 1) * rows
        here = pl.ds(pl.multiple_of(at, 8), rows)
        return jnp.concatenate(
            [ordered[lane, here, :] for lane in range(depth // LANES)], axis=1
        ).astype(jnp.bfloat16)

    for sub in range(subs):
        begin = first[tile * subs + sub]
        own = slice(sub * SUB, (sub + 1) * SUB)
        columns = tile * width + sub * SUB + lax.broadcasted_iota(jnp.int32, (1, SUB), 1)
        products = jnp.dot(
            jnp.concatenate([taken(begin + i) for i in range(HELD)], axis=0),
            legendre[0, :, 0, :, own].reshape(depth, SUB),
            preferred_element_type=jnp.float32,
        )
        total = jnp.where(held(begin, columns), products[0:rows], 0.0)
        for i in range(1, HELD):
            total = total + jnp.where(held(begin + i, columns), products[i * rows : (i + 1) * rows], 0.0)
        mine[:, own] = total[0:kept]
        theirs[:, own] = total[kept:rows].astype(theirs.dtype)

    @pl.loop(0, subs)
    def _(sub):
        begin = first[tile * subs + sub]
        end = last[tile * subs + sub]

        @pl.loop(begin + HELD, end)
        def _(slot):
            own = pl.ds(pl.multiple_of(sub * SUB, SUB), SUB)
            columns = tile * width + sub * SUB + lax.broadcasted_iota(jnp.int32, (1, SUB), 1)
            products = jnp.dot(
                taken(slot),
                legendre[0, :, 0, :, own].reshape(depth, SUB),
                preferred_element_type=jnp.float32,
            )
            inside = held(slot, columns)
            mine[:, own] = jnp.where(inside, products[0:kept], mine[:, own])
            theirs[:, own] = jnp.where(
                inside, products[kept:rows], theirs[:, own].astype(jnp.float32)
            ).astype(theirs.dtype)


def legendre_halves(received, own_waves, legendre, field_count, lat_size, fld_size, rep_size, wave_total):
    slots = own_waves.shape[0]
    counts = jnp.where(own_waves >= 0, wave_total - own_waves, 0)
    lower = lax.broadcasted_iota(jnp.int32, (slots, slots), 1) <= lax.broadcasted_iota(
        jnp.int32, (slots, slots), 0
    )
    stops = jnp.sum(jnp.where(lower, counts[None, :], 0), axis=1)
    starts = stops - counts
    depth, col_count = legendre.shape[1:]
    row_count = depth // (lat_size * rep_size)
    width = min(WIDE, pl.cdiv(col_count, SUB) * SUB)
    tiles = pl.cdiv(col_count, width)
    edges = jnp.arange(tiles * (width // SUB), dtype=jnp.int32)[:, None] * SUB
    first = jnp.sum((stops[None, :] <= edges).astype(jnp.int32), axis=1)
    last = jnp.sum((starts[None, :] < edges + SUB).astype(jnp.int32), axis=1)
    spare = ((0, HELD),)
    rows = fld_size * field_count * 2
    view = legendre.reshape(1, lat_size, rep_size, row_count, col_count)
    return pl.pallas_call(
        functools.partial(legendre_kernel, lat_size, fld_size, field_count),
        out_shape=(
            jax.ShapeDtypeStruct((rows // 2, col_count), jnp.float32),
            jax.ShapeDtypeStruct((rows // 2, col_count), jnp.bfloat16),
        ),
        grid_spec=pltpu.PrefetchScalarGridSpec(
            num_scalar_prefetch=5,
            grid=(tiles,),
            in_specs=[
                pl.BlockSpec(memory_space=pltpu.VMEM),
                pl.BlockSpec(
                    (1, lat_size, 1, row_count, width), lambda t, a, b, c, d, rep: (0, 0, rep[0], 0, t)
                ),
            ],
            out_specs=[
                pl.BlockSpec((rows // 2, width), lambda t, *_: (0, t)),
                pl.BlockSpec((rows // 2, width), lambda t, *_: (0, t)),
            ],
            scratch_shapes=[pltpu.VMEM((depth // rep_size // LANES, slots * rows, LANES), jnp.float32)],
        ),
        compiler_params=pltpu.CompilerParams(vmem_limit_bytes=40 << 20),
    )(
        first, last, jnp.pad(starts, spare), jnp.pad(stops, spare),
        lax.axis_index("rep").reshape(1), received, view,
    )


def pair_kernel(mine, theirs, out, arrived, send_sem, recv_sem):
    lat, fld, rep = lax.axis_index("lat"), lax.axis_index("fld"), lax.axis_index("rep")
    copy = pltpu.make_async_remote_copy(
        src_ref=theirs,
        dst_ref=arrived,
        send_sem=send_sem,
        recv_sem=recv_sem,
        device_id=(lat, fld, 1 - rep),
        device_id_type=pl.DeviceIdType.MESH,
    )
    copy.start()
    copy.wait()
    for level in range(out.shape[1]):
        pair = slice(2 * level, 2 * level + 2)
        out[0, level] = mine[pair, :] + arrived[pair, :].astype(jnp.float32)


def pair_sums(mine, theirs):
    rows, col_count = mine.shape
    in_vmem = pl.BlockSpec(memory_space=pltpu.VMEM)
    return pl.pallas_call(
        pair_kernel,
        out_shape=jax.ShapeDtypeStruct((1, rows // 2, 2, col_count), jnp.float32),
        in_specs=[in_vmem] * 2,
        out_specs=in_vmem,
        scratch_shapes=[
            pltpu.VMEM(theirs.shape, theirs.dtype),
            pltpu.SemaphoreType.DMA,
            pltpu.SemaphoreType.DMA,
        ],
        compiler_params=pltpu.CompilerParams(has_side_effects=True, vmem_limit_bytes=32 << 20),
    )(mine, theirs)


def body(field, wind_zonal, wind_merid, band, waves, legendre):
    field_count, row_count, lon_count = field.shape
    lat_size = lax.axis_size("lat")
    fld_size = lax.axis_size("fld")
    rep_size = lax.axis_size("rep")
    first_row = (lax.axis_index("lat") * rep_size + lax.axis_index("rep")) * row_count
    slot_count = waves.shape[1]
    direct = (
        row_count % 16 == 0
        and slot_count % 16 == 0
        and lon_count % LANES == 0
        and lon_count // LANES <= LANES
        and lon_count % 4 == 0
        and rep_size == 2
        and lat_size % 2 == 0
        and fld_size % 2 == 0
        and fld_size * field_count * 2 % 8 == 0
        and lat_size * row_count % LANES == 0
        and lat_size * fld_size <= 64
    )
    if direct:
        received = spread(
            field, wind_zonal, wind_merid, band, waves, (lat_size, fld_size, rep_size)
        )
        group = lax.axis_index("lat") * fld_size + lax.axis_index("fld")
        own_waves = lax.dynamic_index_in_dim(waves, group, 0, keepdims=False)
        mine, theirs = legendre_halves(
            received, own_waves, legendre, field_count, lat_size, fld_size, rep_size, M
        )
        return pair_sums(mine, theirs)
    bounds = lax.dynamic_slice_in_dim(band, lax.axis_index("fld") * field_count, field_count, 0)
    in_band = band_mask(bounds, first_row, row_count)
    padded = with_halo(field, ((("lat", "rep"), 1),), 1)
    first_section = field + in_band * tendency(
        field, padded[:, 2:], padded[:, :-2], wind_zonal, wind_merid
    )
    padded_section = with_halo(first_section, ((("lat", "rep"), 1),), 1)
    advected = 0.5 * (
        field
        + first_section
        + in_band
        * tendency(
            first_section, padded_section[:, 2:], padded_section[:, :-2], wind_zonal, wind_merid
        )
    )
    grid_low = advected.astype(jnp.bfloat16)
    spectra = jnp.dot(
        grid_low.reshape(field_count * row_count, lon_count),
        dft_matrix(lon_count, M),
        preferred_element_type=jnp.float32,
    ).astype(jnp.bfloat16)
    spectra = spectra.reshape(field_count, row_count, 2, M)
    wave_index = jnp.where(waves >= 0, waves, 0)
    picked = jnp.take(spectra, wave_index.reshape(-1), axis=3)
    picked = picked.reshape(field_count, row_count, 2, lat_size, fld_size, slot_count)
    outgoing = jnp.transpose(picked, (5, 2, 4, 0, 3, 1)).reshape(
        slot_count, 2, fld_size * field_count, lat_size * row_count
    )
    received = lax.all_to_all(
        lax.all_to_all(outgoing, "lat", split_axis=3, concat_axis=3, tiled=True),
        "fld",
        split_axis=2,
        concat_axis=2,
        tiled=True,
    )
    group = lax.axis_index("lat") * fld_size + lax.axis_index("fld")
    own_waves = lax.dynamic_index_in_dim(waves, group, 0, keepdims=False)
    counts = jnp.where(own_waves >= 0, M - own_waves, 0)
    offsets = jnp.cumsum(counts) - counts
    col_count = legendre.shape[2]
    col_ids = lax.broadcasted_iota(jnp.int32, (slot_count, col_count), 1)
    segments = ((col_ids >= offsets[:, None]) & (col_ids < (offsets + counts)[:, None])).astype(
        jnp.float32
    )
    total_fields = fld_size * field_count
    regrouped = lax.all_to_all(received, "rep", split_axis=2, concat_axis=3, tiled=True)
    half_fields = total_fields // rep_size
    ordered = regrouped.reshape(slot_count, 2, half_fields, rep_size, lat_size, row_count)
    ordered = jnp.transpose(ordered, (0, 1, 2, 4, 3, 5)).reshape(
        slot_count * 2 * half_fields, rep_size * lat_size * row_count
    )
    products = jnp.dot(ordered, legendre[0], preferred_element_type=jnp.float32)
    spectrum = jnp.einsum(
        "scfk,sk->fck", products.reshape(slot_count, 2, half_fields, col_count), segments
    )
    return spectrum[None]


def solution(mesh):
    placed = (
        P("fld", ("lat", "rep"), None),
        P("fld", ("lat", "rep"), None),
        P("fld", ("lat", "rep"), None),
        P(),
        P(),
        P(("lat", "fld"), None, None),
    )
    return jax.shard_map(
        body,
        mesh=mesh,
        in_specs=placed,
        out_specs=P(("lat", "fld"), "rep", None, None),
        check_vma=False,
    )
```

time: 187 us -> 135 us (0.72)
  Pallas kernels: 162 us -> 118 us
  starting transfers between devices: 5.69 us -> 0 us
  other arithmetic: 10.4 us -> 8.38 us
    pallas_call x4 -> x3, Pallas kernels: 162 us -> 118 us  [the longest x1 78.9 us: spread(): pl.pallas_call(functools.partial(spread_kernel, sizes, cuts), out_shape=j...]
    ppermute x2 -> x0, starting transfers between devices: 5.69 us -> none  [the longest x1 3.77 us: advection(): lax.ppermute(jnp.concatenate([field[:, -2:]] + [w[:, -1:] for w in winds]...]
    unnamed x11 -> x4, local copies, waits for them, and re-layouts: 4.55 us -> 3.94 us
  transfers between devices with their start and end apart: 2 -> 0, of which waited for: 0 -> 0; matrix products, arithmetic and copies ran while one was open for 7% -> 0% of each run, Pallas kernels for 0% -> 0%
where the time goes in v1:
time: 135 us; the launch traced here: 134 us
  Pallas kernels  118 us (87%)
  other arithmetic  8.38 us (6%)
  local copies, waits for them, and re-layouts  7.36 us (5%)
    pallas_call x1, Pallas kernels, spread(): pl.pallas_call(functools.partial(spread_kernel, sizes, cuts), out_shape=j...  78.9 us
    pallas_call x1, Pallas kernels, legendre_halves(): pl.pallas_call(functools.partial(legendre_kernel, lat_size, fld_size, fie...  30.6 us
    pallas_call x1, Pallas kernels, pair_sums(): pl.pallas_call(pair_kernel, out_shape=jax.ShapeDtypeStruct((1, rows // 2,...  8.32 us
    mul x1, other arithmetic, cos_sin(): jnp.where(odd, cosine, sine) * sin_sign  5.12 us
    unnamed x4, local copies, waits for them, and re-layouts  3.94 us

profile of v1, /device:TPU:15, one launch (start us, length us, event | category | flops | bytes accessed | tf_op | source)
XLA Modules:
  0.0 133.6 jit_solution(7914070864569780692)
XLA Ops:
  0.0 0.7 fusion.22
  0.7 0.1 select_reduce_fusion
  0.8 0.7 bitcast_subtract_fusion.1
  1.5 0.7 fusion.18
  2.3 0.1 convert_reduce_fusion
  2.4 0.8 copy.8.band
  3.1 0.7 compare_select_fusion
  3.8 0.1 mul.139
  3.9 1.1 fusion.20
  5.0 1.1 fusion.21
  6.1 1.1 fusion.19
  7.2 0.2 maximum_bitcast_fusion
  7.4 0.1 pad_maximum_fusion.edges
  7.5 5.1 %select_multiply_fusion = (f32[1280,128]{1,0:T(8,128)}, f32[1280,128]{1,0:T(8,128)}, f32[1280,128]{1,0:T(8,128)S(1)}, f32[1280,128]{1,0:T(8,128)S(1)}) fusion(s32[128]{0:T(128)S(1)} %and_select_fusion, s32[1280]{0:T(1024)S(1)} %mul.139), kind=kLoop, calls=%fused_computation.22 | loop fusion | flops 24248320 | bytes 2627072 | tf_op jit(solution)/shard_map/mul | solution.py:82
  12.6 78.9 %shard_map.64.received = bf16[16,160,480]{2,1,0:T(8,128)(2,1)} custom-call(s32[12,2]{1,0:T(8,128)S(1)} %copy.8.band, f32[2,3,4,2560]{3,2,1,0:T(4,128)S(1)} %pad_maximum_fusion.edges, f32[1280,128]{1,0:T(8,128)S(1)} %get-tuple-element.17.low_cos, f32[1280,128]{1,0:T(8,128)S(1)} %get-tuple-element.18.low_sin, f32[1280,128]{1,0:T(8,128)} %get-tuple-element.16.high_cos, ...), custom_call_target="tpu_custom_call" | custom-call | tf_op jit(solution)/shard_map/pallas_call | solution.py:326
  91.6 0.0 copy-start
  91.6 1.7 %copy-done = bf16[16,160,480]{2,1,0:T(8,128)(2,1)S(1)} copy-done((bf16[16,160,480]{2,1,0:T(8,128)(2,1)S(1)}, bf16[16,160,480]{2,1,0:T(8,128)(2,1)}, u32[]{:S(2)}) %copy-start) | copy-done | bytes 2457624
  93.3 30.6 %shard_map.65 = (f32[12,51328]{1,0:T(8,128)S(1)}, bf16[12,51328]{1,0:T(8,128)(2,1)S(1)}) custom-call(s32[208]{0:T(256)S(1)} %get-tuple-element.22.first, s32[208]{0:T(256)S(1)} %get-tuple-element.21.last, s32[82]{0:T(128)S(1)} %pad.7.starts, s32[82]{0:T(128)S(1)} %pad.8.stops, s32[1]{0:T(128)} %bitcast.3.own_rep, bf16[16,160,480]{2,1,0:T(8,128)(2,1)S(1)} %copy-done, ...), custom_call_target="tpu_custom_call" | custom-call | tf_op jit(solution)/shard_map/pallas_call | solution.py:451
  123.9 8.3 %shard_map.66 = f32[1,6,2,51328]{3,2,1,0:T(2,128)S(1)} custom-call(f32[12,51328]{1,0:T(8,128)S(1)} %get-tuple-element.7.mine, bf16[12,51328]{1,0:T(8,128)(2,1)S(1)} %get-tuple-element.8.theirs), custom_call_target="tpu_custom_call" | custom-call | tf_op jit(solution)/shard_map/pallas_call | solution.py:499
  132.2 1.4 %copy.10 = f32[1,6,2,51328]{3,2,1,0:T(2,128)} copy(f32[1,6,2,51328]{3,2,1,0:T(2,128)S(1)} %shard_map.66) | data formatting | bytes 4927488
  (5 shorter events, 0.0 us)
Async XLA Ops:
  91.6 1.7 %copy-start = (bf16[16,160,480]{2,1,0:T(8,128)(2,1)S(1)}, bf16[16,160,480]{2,1,0:T(8,128)(2,1)}, u32[]{:S(2)}) copy-start(bf16[16,160,480]{2,1,0:T(8,128)(2,1)} %shard_map.64.received) | copy-start | bytes 7372804
